TPU v7x, 32 devices: a whole 2x2x4 slice. The times are simulated.
32 devices in a mesh: row: 8 (over z, x), col: 4 (over y, core).
Axes of the slice: x: 2, y: 2, z: 4, core: 2. Of those that a mesh axis runs over, the one named last changes fastest.
Arguments:
- tokens: bfloat16 [512, 4096], P('row', 'col'), may hold values from -6 to 6
- gate_weight: bfloat16 [4096, 14336], P('col', 'row'), may hold values from -0.09375 to 0.09375
- up_weight: bfloat16 [4096, 14336], P('col', 'row'), may hold values from -0.09375 to 0.09375
- down_weight: bfloat16 [14336, 4096], P('row', 'col'), may hold values from -0.046875 to 0.046875
- gate_mask: int32 [32, 112], replicated, may hold values 0 or 1
- up_mask: int32 [32, 112], replicated, may hold values 0 or 1
- down_mask: int32 [112, 32], replicated, may hold values 0 or 1
- out_grad: bfloat16 [512, 4096], P('row', 'col'), may hold values from -6 to 6
Outputs:
- mixed: bfloat16 [512, 4096], P('row', 'col')
- input_grad: bfloat16 [512, 4096], P('row', 'col')
- gate_grad: float32 [4096, 14336], P('col', 'row')
- up_grad: float32 [4096, 14336], P('col', 'row')
- down_grad: float32 [14336, 4096], P('row', 'col')
All inputs are finite; a program needn't handle non-finite values.
Results may differ from a plain program's by a relative error of at most 0.0049.
Values may be sent and summed in bfloat16 or wider, within the bound.
No kernel may reach another device: no remote copies, remote signals or barrier semaphores. Data moves between devices by JAX's collectives and lax.ppermute only.
A program may use at most 128 MiB of HBM per device.

v0:
```python
import jax
import jax.numpy as jnp
from jax import lax
from jax.sharding import PartitionSpec as P

BLOCK = 128


def expand_mask(mask, row_start, row_count, col_start, col_count):
    row_block = (row_start + lax.broadcasted_iota(jnp.int32, (row_count, 1), 0)) // BLOCK
    left = (row_block == lax.broadcasted_iota(jnp.int32, (1, mask.shape[0]), 1)).astype(jnp.float32)
    col_block = (col_start + lax.broadcasted_iota(jnp.int32, (1, col_count), 1)) // BLOCK
    right = (lax.broadcasted_iota(jnp.int32, (mask.shape[1], 1), 0) == col_block).astype(
        jnp.float32
    )
    middle = jnp.dot(left, mask.astype(jnp.float32), precision=lax.Precision.HIGHEST)
    return jnp.dot(middle, right, precision=lax.Precision.HIGHEST)


def contract_first(left, right):
    return lax.dot_general(
        left, right, (((0,), (0,)), ((), ())), preferred_element_type=jnp.float32
    )


def contract_last(left, right):
    return lax.dot_general(
        left, right, (((1,), (1,)), ((), ())), preferred_element_type=jnp.float32
    )


def per_device(
    tokens, gate_weight, up_weight, down_weight, gate_mask, up_mask, down_mask, out_grad
):
    row_index = lax.axis_index("row")
    col_index = lax.axis_index("col")
    feat_cols = gate_weight.shape[0]
    unit_cols = gate_weight.shape[1]
    keep_gate = expand_mask(
        gate_mask, col_index * feat_cols, feat_cols, row_index * unit_cols, unit_cols
    )
    keep_up = expand_mask(
        up_mask, col_index * feat_cols, feat_cols, row_index * unit_cols, unit_cols
    )
    keep_down = expand_mask(
        down_mask, row_index * unit_cols, unit_cols, col_index * feat_cols, feat_cols
    )
    zero = jnp.zeros((), jnp.bfloat16)
    kept_both = jnp.concatenate(
        [jnp.where(keep_gate > 0, gate_weight, zero), jnp.where(keep_up > 0, up_weight, zero)],
        axis=1,
    )
    kept_down = jnp.where(keep_down > 0, down_weight, zero)
    gathered = lax.all_gather(tokens, "row", axis=0, tiled=True)
    block = gathered
    both = lax.psum_scatter(
        jnp.dot(block, kept_both, preferred_element_type=jnp.float32),
        "col",
        scatter_dimension=0,
        tiled=True,
    )
    gate = both[:, :unit_cols]
    up_part = both[:, unit_cols:]
    sig = jax.nn.sigmoid(gate)
    hidden = (gate * sig * up_part).astype(jnp.bfloat16)
    hidden_all = lax.all_gather(hidden, "col", axis=0, tiled=True)
    block = hidden_all
    mixed = lax.psum_scatter(
        jnp.dot(block, kept_down, preferred_element_type=jnp.float32),
        "row",
        scatter_dimension=0,
        tiled=True,
    ).astype(jnp.bfloat16)
    grad_all = lax.all_gather(out_grad, "row", axis=0, tiled=True)
    down_grad = keep_down * contract_first(hidden_all, grad_all)
    block = grad_all
    hidden_grad = lax.psum_scatter(
        contract_last(block, kept_down), "col", scatter_dimension=0, tiled=True
    )
    dgate = hidden_grad * up_part * sig * (1.0 + gate * (1.0 - sig))
    dup = hidden_grad * gate * sig
    pre_grad = jnp.concatenate([dgate.astype(jnp.bfloat16), dup.astype(jnp.bfloat16)], axis=1)
    pre_all = lax.all_gather(pre_grad, "col", axis=0, tiled=True)
    weight_both = contract_first(gathered, pre_all)
    gate_grad = keep_gate * weight_both[:, :unit_cols]
    up_grad = keep_up * weight_both[:, unit_cols:]
    block = pre_all
    input_grad = lax.psum_scatter(
        contract_last(block, kept_both), "row", scatter_dimension=0, tiled=True
    ).astype(jnp.bfloat16)
    return (mixed, input_grad, gate_grad, up_grad, down_grad)


def solution(mesh):
    return jax.shard_map(
        per_device,
        mesh=mesh,
        in_specs=(
            P("row", "col"),
            P("col", "row"),
            P("col", "row"),
            P("row", "col"),
            P(),
            P(),
            P(),
            P("row", "col"),
        ),
        out_specs=(
            P("row", "col"),
            P("row", "col"),
            P("col", "row"),
            P("col", "row"),
            P("row", "col"),
        ),
        check_vma=False,
    )
```

profile of v0, /device:TPU:0, one launch (start us, length us, event | category | flops | bytes accessed | tf_op | source)
XLA Modules:
  0.0 412.9 jit_solution(11120879040870394195)
XLA Ops:
  7.2 0.0 all-gather.9.cloned.1.call-start
  7.2 0.7 all-gather.9.cloned.1.call-update
  7.9 0.0 all-gather.5.cloned.1.call-start
  7.9 0.7 all-gather.5.cloned.1.call-update
  8.7 0.0 reduce-scatter.9.cloned.1.call-start
  8.7 1.4 fusion.1
  10.1 5.0 %fusion.11 = f32[1792,1024]{1,0:T(8,128)} fusion(f32[1792,32]{1,0:T(8,128)S(1)} %fusion.1, s32[1024]{0:T(1024)S(1)} %add_select_fusion.1), kind=kOutput, calls=%fused_computation.30 | convolution fusion | flops 704675840 | bytes 7573504 | tf_op jit(solution)/shard_map/dot_general | solution.py:17
  15.2 38.0 %all-gather.9.cloned.1.call-done = bf16[512,1024]{1,0:T(8,128)(2,1)} async-done(((bf16[64,1024]{1,0:T(8,128)(2,1)}), bf16[512,1024]{1,0:T(8,128)(2,1)}) %all-gather.9.cloned.1.call-update) | async-done | bytes 1048592 | tf_op jit(solution)/shard_map/all_gather | solution.py:74
  53.1 8.3 %convolution_bitcast_fusion.2 = f32[512,1792]{0,1:T(8,128)} fusion(bf16[512,1024]{1,0:T(8,128)(2,1)} %all-gather.9.cloned.1.call-done, bf16[1792,1024]{1,0:T(8,128)(2,1)} %param.11, f32[1792,1024]{1,0:T(8,128)} %fusion.11), kind=kOutput, calls=%fused_computation.10 | convolution fusion | flops 1882718208 | bytes 15728640 | tf_op jit(solution)/shard_map/dot_general | solution.py:27
  61.4 0.0 reduce-scatter.9.cloned.1.call-update
  61.4 0.2 reduce-scatter.5.cloned.1.call-start
  61.7 0.5 copy-done.1
  62.1 0.5 fusion.4
  62.6 0.0 copy-done.2
  62.6 0.5 fusion.5
  63.1 0.0 copy-start
  63.1 7.6 %compare_select_fusion.2 = (bf16[1024,1792]{1,0:T(8,128)(2,1)}, f32[1024,1792]{1,0:T(8,128)}) fusion(bf16[1024,1792]{1,0:T(8,128)(2,1)} %param.9, f32[1024,112]{1,0:T(8,128)S(1)} %fusion.5, s32[1792]{0:T(1024)S(1)} %add_select_fusion), kind=kOutput, calls=%fused_computation.6 | convolution fusion | flops 2470121472 | bytes 15145984 | tf_op jit(solution)/shard_map/dot_general | solution.py:17
  70.7 0.0 copy-done
  70.7 5.9 %compare_select_fusion.1 = (bf16[1024,1792]{1,0:T(8,128)(2,1)}, f32[1024,1792]{1,0:T(8,128)}) fusion(bf16[1024,1792]{1,0:T(8,128)(2,1)S(1)} %copy-done, f32[1024,112]{1,0:T(8,128)S(1)} %fusion.4, s32[1792]{0:T(1024)S(1)} %add_select_fusion), kind=kOutput, calls=%fused_computation.5 | convolution fusion | flops 2470121472 | bytes 15145984 | tf_op jit(solution)/shard_map/dot_general | solution.py:17
  76.6 17.7 %all-gather.5.cloned.1.call-done = bf16[512,1024]{1,0:T(8,128)(2,1)} async-done(((bf16[64,1024]{1,0:T(8,128)(2,1)}), bf16[512,1024]{1,0:T(8,128)(2,1)}) %all-gather.5.cloned.1.call-update) | async-done | bytes 1048592 | tf_op jit(solution)/shard_map/all_gather | solution.py:54
  94.3 11.0 %convolution_bitcast_fusion.1 = f32[512,3584]{0,1:T(8,128)} fusion(bf16[512,1024]{1,0:T(8,128)(2,1)} %all-gather.5.cloned.1.call-done, bf16[1024,1792]{1,0:T(8,128)(2,1)} %get-tuple-element.10, bf16[1024,1792]{1,0:T(8,128)(2,1)} %get-tuple-element.12), kind=kOutput, calls=%fused_computation.7 | convolution fusion | flops 3772776448 | bytes 15728640 | tf_op jit(solution)/shard_map/dot_general | solution.py:57
  105.2 0.0 reduce-scatter.5.cloned.1.call-update
  105.3 0.0 all-gather.7.cloned.1.call-start
  105.3 31.3 %reduce-scatter.9.cloned.1.call-done = f32[128,1792]{0,1:T(8,128)} async-done(((f32[512,1792]{0,1:T(8,128)}), f32[128,1792]{0,1:T(8,128)}) %reduce-scatter.9.cloned.1.call-update) | async-done | bytes 917520 | tf_op jit(solution)/shard_map/reduce_scatter | solution.py:77
  136.6 67.0 %reduce-scatter.5.cloned.1.call-done = f32[128,3584]{0,1:T(8,128)} async-done(((f32[512,3584]{0,1:T(8,128)}), f32[128,3584]{0,1:T(8,128)}) %reduce-scatter.5.cloned.1.call-update) | async-done | bytes 1835024 | tf_op jit(solution)/shard_map/reduce_scatter | solution.py:56
  203.7 3.1 multiply_convert_fusion.1
  206.7 0.0 all-gather.7.cloned.1.call-update
  206.8 0.0 all-gather.11.cloned.1.call-start
  206.8 1.0 pad_maximum_fusion.3
  207.8 0.0 all-gather.11.cloned.1.call-update
  207.9 0.0 reduce-scatter.7.cloned.1.call-start
  207.9 20.3 %all-gather.7.cloned.1.call-done = bf16[512,1792]{0,1:T(8,128)(2,1)} async-done(((bf16[128,1792]{0,1:T(8,128)(2,1)}), bf16[512,1792]{0,1:T(8,128)(2,1)}) %all-gather.7.cloned.1.call-update) | async-done | bytes 1835024 | tf_op jit(solution)/shard_map/all_gather | solution.py:66
  228.2 8.2 %fusion.24 = f32[512,1024]{1,0:T(8,128)} fusion(bf16[512,1792]{0,1:T(8,128)(2,1)} %all-gather.7.cloned.1.call-done, bf16[1792,1024]{1,0:T(8,128)(2,1)} %param.11, f32[1792,1024]{1,0:T(8,128)} %fusion.11), kind=kOutput, calls=%fused_computation.55 | convolution fusion | flops 1882718208 | bytes 14942208 | tf_op jit(solution)/shard_map/dot_general | solution.py:69
  236.4 0.0 reduce-scatter.7.cloned.1.call-update
  236.4 0.3 reduce-scatter.11.cloned.1.call-start
  236.7 24.9 %all-gather.11.cloned.1.call-done = bf16[512,3584]{0,1:T(8,128)(2,1)} async-done(((bf16[128,3584]{0,1:T(8,128)(2,1)}), bf16[512,3584]{0,1:T(8,128)(2,1)}) %all-gather.11.cloned.1.call-update) | async-done | bytes 3670032 | tf_op jit(solution)/shard_map/all_gather | solution.py:83
  261.6 9.5 %fusion = f32[512,1024]{1,0:T(8,128)} fusion(bf16[512,3584]{0,1:T(8,128)(2,1)} %all-gather.11.cloned.1.call-done, bf16[1024,1792]{1,0:T(8,128)(2,1)} %get-tuple-element.10, bf16[1024,1792]{1,0:T(8,128)(2,1)} %get-tuple-element.12), kind=kOutput, calls=%fused_computation.8 | convolution fusion | flops 3772776448 | bytes 13107200 | tf_op jit(solution)/shard_map/dot_general | solution.py:27
  271.2 0.0 reduce-scatter.11.cloned.1.call-update
  271.2 0.0 copy-start.3
  271.2 0.0 slice-start.1
  271.2 9.4 %convolution_multiply_fusion = f32[1792,1024]{1,0:T(8,128)} fusion(f32[1792,1024]{1,0:T(8,128)} %fusion.11, bf16[512,1792]{0,1:T(8,128)(2,1)} %all-gather.7.cloned.1.call-done, bf16[512,1024]{1,0:T(8,128)(2,1)} %all-gather.9.cloned.1.call-done), kind=kOutput, calls=%fused_computation.9 | convolution fusion | flops 1880883200 | bytes 17563648 | tf_op jit(solution)/shard_map/dot_general | solution.py:21
  280.6 0.0 copy-done.3
  280.6 7.6 %convolution_bitcast_fusion = f32[1024,3584]{1,0:T(8,128)} fusion(bf16[512,3584]{0,1:T(8,128)(2,1)S(1)} %copy-done.3, bf16[512,1024]{1,0:T(8,128)(2,1)S(1)} %copy-done.4), kind=kOutput, calls=%fused_computation | convolution fusion | flops 3758096384 | bytes 19398656 | tf_op jit(solution)/shard_map/dot_general | solution.py:21
  288.2 14.1 %slice_multiply_fusion = (f32[1024,1792]{1,0:T(8,128)}, f32[1024,1792]{1,0:T(8,128)}) fusion(f32[1024,1792]{1,0:T(8,128)} %get-tuple-element.11, f32[1024,3584]{1,0:T(8,128)} %convolution_bitcast_fusion, f32[1024,1792]{1,0:T(8,128)S(1)} %bitcast.18), kind=kLoop, calls=%fused_computation.1 | loop fusion | flops 3670016 | bytes 44040192 | tf_op jit(solution)/shard_map/mul | solution.py:86
  302.3 31.2 %reduce-scatter.7.cloned.1.call-done = f32[64,1024]{1,0:T(8,128)} async-done(((f32[512,1024]{1,0:T(8,128)}), f32[64,1024]{1,0:T(8,128)}) %reduce-scatter.7.cloned.1.call-update) | async-done | bytes 262160 | tf_op jit(solution)/shard_map/reduce_scatter | solution.py:68
  333.5 1.6 convert_element_type.34
  335.1 69.3 %reduce-scatter.11.cloned.1.call-done = f32[64,1024]{1,0:T(8,128)} async-done(((f32[512,1024]{1,0:T(8,128)}), f32[64,1024]{1,0:T(8,128)}) %reduce-scatter.11.cloned.1.call-update) | async-done | bytes 262160 | tf_op jit(solution)/shard_map/reduce_scatter | solution.py:88
  404.5 1.6 convert_element_type.37
  (10 shorter events, 0.0 us)
Async XLA Ops:
  7.2 46.0 %all-gather.9.cloned.1.call-start = ((), (), s32[]{:S(2)}) async-start(), calls=%async_computation.8 | async-start | bytes 1179648 | tf_op jit(solution)/shard_map/all_gather | solution.py:74
  7.9 86.4 %all-gather.5.cloned.1.call-start = ((), (), s32[]{:S(2)}) async-start(), calls=%async_computation.4 | async-start | bytes 1179648 | tf_op jit(solution)/shard_map/all_gather | solution.py:54
  8.7 128.0 %reduce-scatter.9.cloned.1.call-start = ((), (), s32[]{:S(2)}) async-start(), calls=%async_computation.9 | async-start | bytes 4587520 | tf_op jit(solution)/shard_map/reduce_scatter | solution.py:77
  61.4 0.7 copy-start.1
  61.4 1.2 copy-start.2
  61.4 142.2 %reduce-scatter.5.cloned.1.call-start = ((), (), s32[]{:S(2)}) async-start(), calls=%async_computation.5 | async-start | bytes 9175040 | tf_op jit(solution)/shard_map/reduce_scatter | solution.py:56
  63.1 7.6 %copy-start = (bf16[1024,1792]{1,0:T(8,128)(2,1)S(1)}, bf16[1024,1792]{1,0:T(8,128)(2,1)}, u32[]{:S(2)}) copy-start(bf16[1024,1792]{1,0:T(8,128)(2,1)} %param.10) | copy-start | bytes 11010052
  105.3 123.0 %all-gather.7.cloned.1.call-start = ((), (), s32[]{:S(2)}) async-start(), calls=%async_computation.6 | async-start | bytes 2293760 | tf_op jit(solution)/shard_map/all_gather | solution.py:66
  206.8 54.9 %all-gather.11.cloned.1.call-start = ((), (), s32[]{:S(2)}) async-start(), calls=%async_computation.10 | async-start | bytes 4587520 | tf_op jit(solution)/shard_map/all_gather | solution.py:83
  207.9 125.6 %reduce-scatter.7.cloned.1.call-start = ((), (), s32[]{:S(2)}) async-start(), calls=%async_computation.7 | async-start | bytes 2359296 | tf_op jit(solution)/shard_map/reduce_scatter | solution.py:68
  236.4 168.0 %reduce-scatter.11.cloned.1.call-start = ((), (), s32[]{:S(2)}) async-start(), calls=%async_computation.11 | async-start | bytes 2359296 | tf_op jit(solution)/shard_map/reduce_scatter | solution.py:88
  271.2 17.0 %slice-start = ((s8[7340032]{0:T(1024)(128)(4,1)}), s8[3145728]{0:T(1024)(128)(4,1)S(1)}, s32[]{:S(2)}) async-start(s8[7340032]{0:T(1024)(128)(4,1)} %bitcast.17), calls=%async_computation.12 | async-start | bytes 6291456
  271.2 9.4 %copy-start.3 = (bf16[512,3584]{0,1:T(8,128)(2,1)S(1)}, bf16[512,3584]{0,1:T(8,128)(2,1)}, u32[]{:S(2)}) copy-start(bf16[512,3584]{0,1:T(8,128)(2,1)} %all-gather.11.cloned.1.call-done) | copy-start | bytes 11010052
  271.2 9.4 %copy-start.4 = (bf16[512,1024]{1,0:T(8,128)(2,1)S(1)}, bf16[512,1024]{1,0:T(8,128)(2,1)}, u32[]{:S(2)}) copy-start(bf16[512,1024]{1,0:T(8,128)(2,1)} %all-gather.5.cloned.1.call-done) | copy-start | bytes 3145732
  271.2 17.0 %slice-start.1 = ((s8[7340032]{0:T(1024)(128)(4,1)}), s8[4194304]{0:T(1024)(128)(4,1)S(1)}, s32[]{:S(2)}) async-start(s8[7340032]{0:T(1024)(128)(4,1)} %bitcast.17), calls=%async_computation.13 | async-start | bytes 8388608
Sparse Core Ops, SparseCore 0:
  10.1 42.9 all-gather.8
  55.3 38.9 all-gather.4
  96.8 39.7 reduce-scatter.8
  139.0 64.6 reduce-scatter.4
  206.9 21.3 all-gather.6
  229.6 31.9 all-gather.10
  265.2 68.2 reduce-scatter.6
  337.0 67.3 reduce-scatter.10
where the time goes:
time: 413 us
  waiting for transfers between devices  301 us (73%)
  matrix products  74.7 us (18%)
  other arithmetic  21.4 us (5%)
  between operations  14.2 us (3%)
    reduce_scatter x1, waiting for transfers between devices, per_device(): lax.psum_scatter(contract_last(block, kept_both), 'row', scatter_dimensio...  69.3 us
    reduce_scatter x1, waiting for transfers between devices, per_device(): lax.psum_scatter(jnp.dot(block, kept_both, preferred_element_type=jnp.flo...  67 us
    all_gather x1, waiting for transfers between devices, per_device(): grad_all = lax.all_gather(out_grad, 'row', axis=0, tiled=True)  38 us
    reduce_scatter x1, waiting for transfers between devices, per_device(): lax.psum_scatter(contract_last(block, kept_down), 'col', scatter_dimensio...  31.3 us
    reduce_scatter x1, waiting for transfers between devices, per_device(): lax.psum_scatter(jnp.dot(block, kept_down, preferred_element_type=jnp.flo...  31.2 us
    all_gather x1, waiting for transfers between devices, per_device(): pre_all = lax.all_gather(pre_grad, 'col', axis=0, tiled=True)  24.9 us
    all_gather x1, waiting for transfers between devices, per_device(): hidden_all = lax.all_gather(hidden, 'col', axis=0, tiled=True)  20.3 us
    dot_general x3, matrix products, expand_mask(): return jnp.dot(middle, right, precision=lax.Precision.HIGHEST)  18.6 us
  transfers between devices with their start and end apart: 8, of which 8 were waited for; matrix products, arithmetic and copies ran while one was open for 22% of the time, Pallas kernels for 0%

commit v1 on v0

--- a/solution.py
+++ b/solution.py
@@ -80,7 +80,14 @@
     dgate = hidden_grad * up_part * sig * (1.0 + gate * (1.0 - sig))
     dup = hidden_grad * gate * sig
     pre_grad = jnp.concatenate([dgate.astype(jnp.bfloat16), dup.astype(jnp.bfloat16)], axis=1)
-    pre_all = lax.all_gather(pre_grad, "col", axis=0, tiled=True)
+    ways, here, step = (lax.axis_size("col"), lax.axis_index("col"), pre_grad.shape[0])
+    line, have = (pre_grad, 1)
+    while have < ways:
+        line = jnp.concatenate(
+            [line, lax.ppermute(line, "col", [(d, (d - have) % ways) for d in range(ways)])], axis=0
+        )
+        have = 2 * have
+    pre_all = jnp.roll(line, here * step, axis=0)
     weight_both = contract_first(gathered, pre_all)
     gate_grad = keep_gate * weight_both[:, :unit_cols]
     up_grad = keep_up * weight_both[:, unit_cols:]

time: 413 us -> 389 us (0.942)
  waiting for transfers between devices: 301 us -> 269 us
  local copies, waits for them, and re-layouts: 0.49 us -> 5.49 us
  other arithmetic: 21.4 us -> 26.1 us
    ppermute x0 -> x2, waiting for transfers between devices: none -> 49.6 us  [per_device(): lax.ppermute(line, 'col', [(d, (d - have) % ways) for d in range(ways)])]
    reduce_scatter x1, waiting for transfers between devices: 31.2 us -> 0.01 us  [per_device(): lax.psum_scatter(jnp.dot(block, kept_down, preferred_element_type=jnp.flo...]
    all_gather x1 -> x0, waiting for transfers between devices: 24.9 us -> none  [per_device(): pre_all = lax.all_gather(pre_grad, 'col', axis=0, tiled=True)]
    all_gather x1, waiting for transfers between devices: 20.3 us -> 2.79 us  [per_device(): hidden_all = lax.all_gather(hidden, 'col', axis=0, tiled=True)]
    reduce_scatter x1, waiting for transfers between devices: 69.3 us -> 60.9 us  [per_device(): lax.psum_scatter(contract_last(block, kept_both), 'row', scatter_dimensio...]
  transfers between devices with their start and end apart: 8 -> 9, of which waited for: 8 -> 8; matrix products, arithmetic and copies ran while one was open for 22% -> 25% of each run, Pallas kernels for 0% -> 0%
where the time goes in v1:
time: 389 us; the launch traced here: 388 us
  waiting for transfers between devices  269 us (69%)
  matrix products  72.6 us (19%)
  other arithmetic  26.1 us (7%)
  between operations  14.3 us (4%)
  local copies, waits for them, and re-layouts  5.49 us (1%)
    reduce_scatter x1, waiting for transfers between devices, per_device(): lax.psum_scatter(jnp.dot(block, kept_both, preferred_element_type=jnp.flo...  67 us
    reduce_scatter x1, waiting for transfers between devices, per_device(): lax.psum_scatter(contract_last(block, kept_both), 'row', scatter_dimensio...  60.9 us
    ppermute x2, waiting for transfers between devices, per_device(): lax.ppermute(line, 'col', [(d, (d - have) % ways) for d in range(ways)])  49.6 us
    all_gather x1, waiting for transfers between devices, per_device(): grad_all = lax.all_gather(out_grad, 'row', axis=0, tiled=True)  38 us
    reduce_scatter x1, waiting for transfers between devices, per_device(): lax.psum_scatter(contract_last(block, kept_down), 'col', scatter_dimensio...  31.3 us
    dot_general x3, matrix products, expand_mask(): return jnp.dot(middle, right, precision=lax.Precision.HIGHEST)  18.6 us
    all_gather x1, waiting for transfers between devices, per_device(): gathered = lax.all_gather(tokens, 'row', axis=0, tiled=True)  17.7 us
    dot_general x2, matrix products, contract_first(): lax.dot_general(left, right, (((0,), (0,)), ((), ())), preferred_element_...  16.8 us
  transfers between devices with their start and end apart: 9, of which 8 were waited for; matrix products, arithmetic and copies ran while one was open for 25% of the time, Pallas kernels for 0%

profile of v1, /device:TPU:0, one launch (start us, length us, event | category | flops | bytes accessed | tf_op | source)
XLA Modules:
  0.0 388.4 jit_solution(2181843242203250253)
XLA Ops:
  7.2 0.0 all-gather.8.cloned.1.call-start
  7.2 0.7 all-gather.8.cloned.1.call-update
  7.9 0.0 all-gather.4.cloned.1.call-start
  7.9 0.7 all-gather.4.cloned.1.call-update
  8.7 0.0 reduce-scatter.9.cloned.1.call-start
  8.7 1.4 fusion.3
  10.1 5.0 %fusion.13 = f32[1792,1024]{1,0:T(8,128)} fusion(f32[1792,32]{1,0:T(8,128)S(1)} %fusion.3, s32[1024]{0:T(1024)S(1)} %add_select_fusion.1), kind=kOutput, calls=%fused_computation.33 | convolution fusion | flops 704675840 | bytes 7573504 | tf_op jit(solution)/shard_map/dot_general | solution.py:17
  15.2 38.0 %all-gather.8.cloned.1.call-done = bf16[512,1024]{1,0:T(8,128)(2,1)} async-done(((bf16[64,1024]{1,0:T(8,128)(2,1)}), bf16[512,1024]{1,0:T(8,128)(2,1)}) %all-gather.8.cloned.1.call-update) | async-done | bytes 1048592 | tf_op jit(solution)/shard_map/all_gather | solution.py:74
  53.1 8.3 %convolution_bitcast_fusion.2 = f32[512,1792]{0,1:T(8,128)} fusion(bf16[512,1024]{1,0:T(8,128)(2,1)} %all-gather.8.cloned.1.call-done, bf16[1792,1024]{1,0:T(8,128)(2,1)} %param.11, f32[1792,1024]{1,0:T(8,128)} %fusion.13), kind=kOutput, calls=%fused_computation.10 | convolution fusion | flops 1882718208 | bytes 15728640 | tf_op jit(solution)/shard_map/dot_general | solution.py:27
  61.4 0.0 reduce-scatter.9.cloned.1.call-update
  61.4 0.2 reduce-scatter.5.cloned.1.call-start
  61.7 0.5 copy-done.7
  62.1 0.5 fusion.6
  62.6 0.5 fusion.7
  63.1 0.0 copy-start.4
  63.1 7.6 %compare_select_fusion.2 = (bf16[1024,1792]{1,0:T(8,128)(2,1)}, f32[1024,1792]{1,0:T(8,128)}) fusion(bf16[1024,1792]{1,0:T(8,128)(2,1)} %param.9, f32[1024,112]{1,0:T(8,128)S(1)} %fusion.7, s32[1792]{0:T(1024)S(1)} %add_select_fusion), kind=kOutput, calls=%fused_computation.6 | convolution fusion | flops 2470121472 | bytes 15145984 | tf_op jit(solution)/shard_map/dot_general | solution.py:17
  70.7 5.9 %compare_select_fusion.1 = (bf16[1024,1792]{1,0:T(8,128)(2,1)}, f32[1024,1792]{1,0:T(8,128)}) fusion(bf16[1024,1792]{1,0:T(8,128)(2,1)S(1)} %copy-done.4, f32[1024,112]{1,0:T(8,128)S(1)} %fusion.6, s32[1792]{0:T(1024)S(1)} %add_select_fusion), kind=kOutput, calls=%fused_computation.5 | convolution fusion | flops 2470121472 | bytes 15145984 | tf_op jit(solution)/shard_map/dot_general | solution.py:17
  76.6 17.7 %all-gather.4.cloned.1.call-done = bf16[512,1024]{1,0:T(8,128)(2,1)} async-done(((bf16[64,1024]{1,0:T(8,128)(2,1)}), bf16[512,1024]{1,0:T(8,128)(2,1)}) %all-gather.4.cloned.1.call-update) | async-done | bytes 1048592 | tf_op jit(solution)/shard_map/all_gather | solution.py:54
  94.3 11.0 %convolution_bitcast_fusion.1 = f32[512,3584]{0,1:T(8,128)} fusion(bf16[512,1024]{1,0:T(8,128)(2,1)} %all-gather.4.cloned.1.call-done, bf16[1024,1792]{1,0:T(8,128)(2,1)} %get-tuple-element.12, bf16[1024,1792]{1,0:T(8,128)(2,1)} %get-tuple-element.14), kind=kOutput, calls=%fused_computation.7 | convolution fusion | flops 3772776448 | bytes 15728640 | tf_op jit(solution)/shard_map/dot_general | solution.py:57
  105.2 0.0 reduce-scatter.5.cloned.1.call-update
  105.3 0.0 all-gather.6.cloned.1.call-start
  105.3 31.3 %reduce-scatter.9.cloned.1.call-done = f32[128,1792]{0,1:T(8,128)} async-done(((f32[512,1792]{0,1:T(8,128)}), f32[128,1792]{0,1:T(8,128)}) %reduce-scatter.9.cloned.1.call-update) | async-done | bytes 917520 | tf_op jit(solution)/shard_map/reduce_scatter | solution.py:77
  136.6 67.0 %reduce-scatter.5.cloned.1.call-done = f32[128,3584]{0,1:T(8,128)} async-done(((f32[512,3584]{0,1:T(8,128)}), f32[128,3584]{0,1:T(8,128)}) %reduce-scatter.5.cloned.1.call-update) | async-done | bytes 1835024 | tf_op jit(solution)/shard_map/reduce_scatter | solution.py:56
  203.7 3.0 multiply_convert_fusion.1
  206.7 0.0 all-gather.6.cloned.1.call-update
  206.8 0.0 reduce-scatter.7.cloned.1.call-start
  206.8 1.1 pad_maximum_fusion.4
  207.9 19.5 %collective-permute-done = bf16[128,3584]{0,1:T(8,128)(2,1)S(1)} collective-permute-done((bf16[128,3584]{0,1:T(8,128)(2,1)S(1)}, bf16[128,3584]{0,1:T(8,128)(2,1)S(1)}, u32[]{:S(2)}, u32[]{:S(2)}) %collective-permute-start) | collective-permute-done | bytes 917536 | tf_op jit(solution)/shard_map/ppermute | solution.py:87
  227.4 1.5 pad_maximum_fusion.3
  228.9 0.4 collective-permute-start.1
  229.4 2.8 all-gather.6.cloned.1.call-done
  232.2 8.2 %fusion.28 = f32[512,1024]{1,0:T(8,128)} fusion(bf16[512,1792]{0,1:T(8,128)(2,1)} %all-gather.6.cloned.1.call-done, bf16[1792,1024]{1,0:T(8,128)(2,1)} %param.11, f32[1792,1024]{1,0:T(8,128)} %fusion.13), kind=kOutput, calls=%fused_computation.66 | convolution fusion | flops 1882718208 | bytes 14942208 | tf_op jit(solution)/shard_map/dot_general | solution.py:69
  240.3 0.0 reduce-scatter.7.cloned.1.call-update
  240.4 0.3 reduce-scatter.11.cloned.1.call-start
  240.7 1.1 constant_dynamic-update-slice_fusion.4
  241.7 30.2 %collective-permute-done.1 = bf16[256,3584]{0,1:T(8,128)(2,1)S(1)} collective-permute-done((bf16[256,3584]{0,1:T(8,128)(2,1)}, bf16[256,3584]{0,1:T(8,128)(2,1)S(1)}, u32[]{:S(2)}, u32[]{:S(2)}) %collective-permute-start.1) | collective-permute-done | bytes 1835040 | tf_op jit(solution)/shard_map/ppermute | solution.py:87
  271.9 1.4 constant_dynamic-update-slice_fusion.3
  273.3 1.0 constant_dynamic-update-slice_fusion.2
  274.3 1.1 constant_dynamic-update-slice_fusion.1
  275.4 1.4 constant_dynamic-update-slice_fusion
  276.8 7.5 %fusion = f32[512,1024]{1,0:T(8,128)} fusion(bf16[1024,1792]{1,0:T(8,128)(2,1)S(1)} %copy-done.6, bf16[1024,1792]{1,0:T(8,128)(2,1)S(1)} %copy-done.5, bf16[1024,3584]{0,1:T(8,128)(2,1)} %constant_dynamic-update-slice_fusion, s32[]{:T(128)S(6)} %select_n.68), kind=kOutput, calls=%fused_computation.8 | convolution fusion | flops 3772776448 | bytes 13107204 | tf_op jit(solution)/shard_map/dot_general | solution.py:27
  284.3 0.0 reduce-scatter.11.cloned.1.call-update
  284.3 11.7 %convolution_bitcast_fusion = f32[1024,3584]{1,0:T(8,128)} fusion(bf16[512,1024]{1,0:T(8,128)(2,1)} %all-gather.4.cloned.1.call-done, bf16[1024,3584]{0,1:T(8,128)(2,1)} %constant_dynamic-update-slice_fusion, s32[]{:T(128)S(6)} %select_n.68), kind=kOutput, calls=%fused_computation | convolution fusion | flops 3758096384 | bytes 19398660 | tf_op jit(solution)/shard_map/dot_general | solution.py:21
  296.1 5.1 %convolution_multiply_fusion = f32[1792,1024]{1,0:T(8,128)} fusion(f32[1792,1024]{1,0:T(8,128)S(1)} %bitcast.16, bf16[512,1792]{0,1:T(8,128)(2,1)S(1)} %copy-done.2, bf16[512,1024]{1,0:T(8,128)(2,1)S(1)} %copy-done.3), kind=kOutput, calls=%fused_computation.9 | convolution fusion | flops 1880883200 | bytes 17563648 | tf_op jit(solution)/shard_map/dot_general | solution.py:21
  301.2 16.2 %slice_multiply_fusion = (f32[1024,1792]{1,0:T(8,128)}, f32[1024,1792]{1,0:T(8,128)}) fusion(f32[1024,1792]{1,0:T(8,128)} %get-tuple-element.13, f32[1024,3584]{1,0:T(8,128)} %convolution_bitcast_fusion, f32[1024,1792]{1,0:T(8,128)} %get-tuple-element.15), kind=kLoop, calls=%fused_computation.1 | loop fusion | flops 3670016 | bytes 44040192 | tf_op jit(solution)/shard_map/mul | solution.py:93
  317.4 1.6 convert_element_type.34
  319.0 60.9 %reduce-scatter.11.cloned.1.call-done = f32[64,1024]{1,0:T(8,128)} async-done(((f32[512,1024]{1,0:T(8,128)}), f32[64,1024]{1,0:T(8,128)}) %reduce-scatter.11.cloned.1.call-update) | async-done | bytes 262160 | tf_op jit(solution)/shard_map/reduce_scatter | solution.py:95
  379.9 1.6 convert_element_type.37
  (25 shorter events, 0.1 us)
Async XLA Ops:
  7.2 46.0 %all-gather.8.cloned.1.call-start = ((), (), s32[]{:S(2)}) async-start(), calls=%async_computation.8 | async-start | bytes 1179648 | tf_op jit(solution)/shard_map/all_gather | solution.py:74
  7.9 86.4 %all-gather.4.cloned.1.call-start = ((), (), s32[]{:S(2)}) async-start(), calls=%async_computation.4 | async-start | bytes 1179648 | tf_op jit(solution)/shard_map/all_gather | solution.py:54
  8.7 128.0 %reduce-scatter.9.cloned.1.call-start = ((), (), s32[]{:S(2)}) async-start(), calls=%async_computation.9 | async-start | bytes 4587520 | tf_op jit(solution)/shard_map/reduce_scatter | solution.py:77
  61.4 0.7 copy-start.7
  61.4 1.2 copy-start.8
  61.4 142.2 %reduce-scatter.5.cloned.1.call-start = ((), (), s32[]{:S(2)}) async-start(), calls=%async_computation.5 | async-start | bytes 9175040 | tf_op jit(solution)/shard_map/reduce_scatter | solution.py:56
  63.1 7.6 %copy-start.4 = (bf16[1024,1792]{1,0:T(8,128)(2,1)S(1)}, bf16[1024,1792]{1,0:T(8,128)(2,1)}, u32[]{:S(2)}) copy-start(bf16[1024,1792]{1,0:T(8,128)(2,1)} %param.10) | copy-start | bytes 11010052
  105.3 126.9 %all-gather.6.cloned.1.call-start = ((), (), s32[]{:S(2)}) async-start(), calls=%async_computation.6 | async-start | bytes 2293760 | tf_op jit(solution)/shard_map/all_gather | solution.py:66
  206.7 20.7 %copy-start = (bf16[128,1792]{0,1:T(8,128)(2,1)}, bf16[128,1792]{0,1:T(8,128)(2,1)S(1)}, u32[]{:S(2)}) copy-start(bf16[128,1792]{0,1:T(8,128)(2,1)S(1)} %get-tuple-element.8) | copy-start | bytes 1376260
  206.8 110.6 %reduce-scatter.7.cloned.1.call-start = ((), (), s32[]{:S(2)}) async-start(), calls=%async_computation.7 | async-start | bytes 2359296 | tf_op jit(solution)/shard_map/reduce_scatter | solution.py:68
  207.9 19.5 %collective-permute-start = (bf16[128,3584]{0,1:T(8,128)(2,1)S(1)}, bf16[128,3584]{0,1:T(8,128)(2,1)S(1)}, u32[]{:S(2)}, u32[]{:S(2)}) collective-permute-start(bf16[128,3584]{0,1:T(8,128)(2,1)S(1)} %get-tuple-element.10), channel_id=1, source_target_pairs={{0,3},{1,0},{2,1},{3,2},{4,7},{5,4},{6,5},{7,6},{8,11},{9,8},{10,9... | collective-permute-start | bytes 2752520 | tf_op jit(solution)/shard_map/ppermute | solution.py:87
  228.9 42.9 %collective-permute-start.1 = (bf16[256,3584]{0,1:T(8,128)(2,1)}, bf16[256,3584]{0,1:T(8,128)(2,1)S(1)}, u32[]{:S(2)}, u32[]{:S(2)}) collective-permute-start(bf16[256,3584]{0,1:T(8,128)(2,1)} %pad_maximum_fusion.3), channel_id=1, source_target_pairs={{0,2},{1,3},{2,0},{3,1},{4,6},{5,7},{6,4},{7,5},{8,10},{9,11},{10,... | collective-permute-start | bytes 5505032 | tf_op jit(solution)/shard_map/ppermute | solution.py:87
  240.4 139.6 %reduce-scatter.11.cloned.1.call-start = ((), (), s32[]{:S(2)}) async-start(), calls=%async_computation.10 | async-start | bytes 2359296 | tf_op jit(solution)/shard_map/reduce_scatter | solution.py:95
  240.6 32.7 %copy-start.1 = (bf16[128,1792]{0,1:T(8,128)(2,1)S(1)}, bf16[128,1792]{0,1:T(8,128)(2,1)}, u32[]{:S(2)}) copy-start(bf16[128,1792]{0,1:T(8,128)(2,1)} %copy-done) | copy-start | bytes 1376260
  271.9 4.9 %copy-start.6 = (bf16[1024,1792]{1,0:T(8,128)(2,1)S(1)}, bf16[1024,1792]{1,0:T(8,128)(2,1)}, u32[]{:S(2)}) copy-start(bf16[1024,1792]{1,0:T(8,128)(2,1)} %get-tuple-element.12) | copy-start | bytes 11010052
  273.3 3.5 copy-start.5
  284.3 11.8 %slice-start = ((s8[7340032]{0:T(1024)(128)(4,1)}), s8[3145728]{0:T(1024)(128)(4,1)S(1)}, s32[]{:S(2)}) async-start(s8[7340032]{0:T(1024)(128)(4,1)} %bitcast.15), calls=%async_computation.11 | async-start | bytes 6291456
  284.3 11.8 %slice-start.1 = ((s8[7340032]{0:T(1024)(128)(4,1)}), s8[4194304]{0:T(1024)(128)(4,1)S(1)}, s32[]{:S(2)}) async-start(s8[7340032]{0:T(1024)(128)(4,1)} %bitcast.15), calls=%async_computation.12 | async-start | bytes 8388608
  284.3 11.7 %copy-start.2 = (bf16[512,1792]{0,1:T(8,128)(2,1)S(1)}, bf16[512,1792]{0,1:T(8,128)(2,1)}, u32[]{:S(2)}) copy-start(bf16[512,1792]{0,1:T(8,128)(2,1)} %all-gather.6.cloned.1.call-done) | copy-start | bytes 5505028
  284.3 11.7 %copy-start.3 = (bf16[512,1024]{1,0:T(8,128)(2,1)S(1)}, bf16[512,1024]{1,0:T(8,128)(2,1)}, u32[]{:S(2)}) copy-start(bf16[512,1024]{1,0:T(8,128)(2,1)} %all-gather.8.cloned.1.call-done) | copy-start | bytes 3145732
Sparse Core Ops, SparseCore 0:
  10.1 42.9 all-gather.7
  55.3 38.9 all-gather.3
  96.8 39.7 reduce-scatter.8
  139.0 64.6 reduce-scatter.4
  206.9 25.2 all-gather.5
  240.5 68.3 reduce-scatter.6
  312.4 67.4 reduce-scatter.10
